TPU v7x, 128 devices: a whole 4x4x4 slice. The times are simulated.
128 devices in a mesh: date: 8 (over y, core), strip: 16 (over z, x).
Axes of the slice: x: 4, y: 4, z: 4, core: 2. Of those that a mesh axis runs over, the one named last changes fastest.
Arguments:
- stack: float32 [64, 1024, 2048], P('date', 'strip'), may hold values from -6 to 6
- spatial_taps: float32 [13], replicated, may hold values from 0.2 to 1
- temporal_taps: float32 [2, 5], replicated, may hold values from -0.25 to 0.25
- foot_tile: int32 [16384], P(('date', 'strip')), may hold values from 0 to 1
- foot_row: int32 [16384], P(('date', 'strip')), may hold values from 0 to 63
- foot_count: int32 [16384], P(('date', 'strip')), may hold values from 1 to 128
- foot_owner: int32 [16384, 1], P(('date', 'strip')), may hold values from 0 to 127; in each aligned block of 128 rows (0 to 127, 128 to 255, ...) at most 2 rows name the same one
Outputs:
- residual: float32 [64, 1024, 2048], P(None, 'strip', 'date')
- anomaly: float32 [128, 256, 64], P(('date', 'strip'))
- asset_series: float32 [128, 64], P(('date', 'strip'))
Inputs may be any that keep to these rules, and one draw needn't show every extreme that they name: `foot_owner`: among the footprints of one block, no owner appears more than 2 times, a bound that some block reaches; every owner has some footprint.
All inputs are finite; a program needn't handle non-finite values.
Results may differ from a plain program's by a relative error of at most 0.000075.
Values sent between devices are 32-bit elements; how exact they have to be, the bound alone decides.
A program may use at most 128 MiB of HBM per device.

v0:
```python
import jax
import jax.numpy as jnp
from jax import lax
from jax.sharding import PartitionSpec as P

TILE = 128
RADIUS = 6
REACH = 2
DILATION = 8
PAIR_CAP = 2


def with_halo(value, sides, width):
    for axis, dim in sides:
        peers, length = (lax.axis_size(axis), value.shape[dim])
        up = [(i, (i + 1) % peers) for i in range(peers - 1)]
        down = [(j, i) for i, j in up]
        last = lax.slice_in_dim(value, length - width, length, axis=dim)
        initial = lax.slice_in_dim(value, 0, width, axis=dim)
        before = lax.ppermute(last, axis, up)
        after = lax.ppermute(initial, axis, down)
        value = jnp.concatenate([before, value, after], axis=dim)
    return value


def taps_pass(padded, weights, axis_num, length):
    summed = weights[0] * lax.slice_in_dim(padded, 0, length, axis=axis_num)
    for k in range(1, weights.shape[0]):
        summed = summed + weights[k] * lax.slice_in_dim(padded, k, k + length, axis=axis_num)
    return summed


def temporal_filter(series, temporal_taps):
    date_count = series.shape[0]
    for level_idx, spacing in enumerate((1, DILATION)):
        margin = REACH * spacing
        padded = jnp.pad(series, ((margin, margin), (0, 0), (0, 0)))
        smooth_part = temporal_taps[level_idx, 0] * lax.slice_in_dim(padded, 0, date_count, axis=0)
        for k in range(1, 2 * REACH + 1):
            smooth_part = smooth_part + temporal_taps[level_idx, k] * lax.slice_in_dim(
                padded, k * spacing, k * spacing + date_count, axis=0
            )
        series = series - smooth_part
    return series


def shards(stack, spatial_taps, temporal_taps, foot_tile, foot_row, foot_count, foot_owner):
    weights = spatial_taps / jnp.sum(spatial_taps)
    padded = jnp.pad(stack, ((0, 0), (0, 0), (RADIUS, RADIUS)))
    across = taps_pass(padded, weights, 2, stack.shape[2])
    rimmed = with_halo(across, (("strip", 1),), RADIUS)
    corrected = stack - taps_pass(rimmed, weights, 1, stack.shape[1])
    residual = temporal_filter(
        lax.all_to_all(corrected, "date", split_axis=2, concat_axis=0, tiled=True), temporal_taps
    )
    date_count, row_count, col_count = residual.shape
    tile_view = residual.reshape(date_count, row_count, col_count // TILE, TILE)
    picked = tile_view[:, foot_row, foot_tile, :]
    counts = foot_count.astype(jnp.float32)
    inside = (jnp.arange(TILE, dtype=jnp.int32)[None, :] < foot_count[:, None]).astype(jnp.float32)
    foot_mean = jnp.sum(picked * inside[None], axis=2) / counts[None, :]
    owners = foot_owner[:, 0]
    position = jnp.arange(owners.shape[0], dtype=jnp.int32)
    earlier = (owners[:, None] == owners[None, :]) & (position[None, :] < position[:, None])
    slot_rank = jnp.sum(earlier.astype(jnp.int32), axis=1)
    date_devices = lax.axis_size("date")
    strip_devices = lax.axis_size("strip")
    devices_all = date_devices * strip_devices
    dest_slot = owners * PAIR_CAP + slot_rank
    onehot = (
        dest_slot[:, None] == jnp.arange(devices_all * PAIR_CAP, dtype=jnp.int32)[None, :]
    ).astype(jnp.float32)
    outgoing = jnp.einsum("fk,tf->kt", onehot, foot_mean, precision=lax.Precision.HIGHEST)
    out_weight = jnp.einsum("fk,f->k", onehot, counts, precision=lax.Precision.HIGHEST)
    received, weight_in = (
        lax.all_to_all(
            outgoing.reshape(devices_all, PAIR_CAP, date_count),
            ("date", "strip"),
            split_axis=0,
            concat_axis=0,
            tiled=True,
        ),
        lax.all_to_all(
            out_weight.reshape(devices_all, PAIR_CAP),
            ("date", "strip"),
            split_axis=0,
            concat_axis=0,
            tiled=True,
        ),
    )
    total_weight = jnp.sum(weight_in)
    asset_mean = jnp.sum(weight_in[:, :, None] * received, axis=(0, 1)) / total_weight
    anomaly = jnp.where(weight_in[:, :, None] > 0, received - asset_mean[None, None, :], 0.0)
    return (residual, anomaly.reshape(1, devices_all * PAIR_CAP, date_count), asset_mean[None, :])


def solution(mesh):
    placed = (
        P("date", "strip", None),
        P(),
        P(),
        P(("date", "strip")),
        P(("date", "strip")),
        P(("date", "strip")),
        P(("date", "strip"), None),
    )
    return jax.shard_map(
        shards,
        mesh=mesh,
        in_specs=placed,
        out_specs=(
            P(None, "strip", "date"),
            P(("date", "strip"), None, None),
            P(("date", "strip"), None),
        ),
        check_vma=False,
    )
```

profile of v0, /device:TPU:1, one launch (start us, length us, event | category | flops | bytes accessed | tf_op | source)
XLA Modules:
  0.0 279.2 jit_solution(2231093077993058063)
XLA Ops:
  0.6 1.3 reduce_sum.47
  1.9 1.3 broadcast_divide_fusion.1
  3.2 0.7 fusion.75
  3.9 6.6 %copy.37 = f32[8,64,2048]{2,0,1:T(8,128)} copy(f32[8,64,2048]{2,1,0:T(8,128)} %param.7) | data formatting | bytes 8388608 | tf_op args[0]
  10.5 42.0 %multiply_add_fusion = f32[8,64,2048]{2,0,1:T(8,128)} fusion(f32[8,64,2048]{2,0,1:T(8,128)} %copy.37, f32[]{:T(128)} %bitcast.12, f32[]{:T(128)} %bitcast.11, f32[]{:T(128)} %bitcast.10, f32[]{:T(128)} %bitcast.9, f32[]{:T(128)} %bitcast.8, f32[]{:T(128)} %bitcast.7, f32[]{:T(128)} %bitcast.6, f32[]{:T(128)} %bitcast.5, f32[]{:T(128)} %bitcast.4, ...), kind=kLoop, calls=%fused_computation.79 | loop fusion | flops 26214400 | bytes 8388660 | tf_op jit(solution)/shard_map/add | solution.py:29
  52.6 1.2 fusion.73
  53.7 4.0 %collective-permute-start = (f32[8,6,2048]{2,0,1:T(8,128)S(1)}, f32[8,6,2048]{2,0,1:T(8,128)S(1)}, u32[]{:S(2)}, u32[]{:S(2)}) collective-permute-start(f32[8,6,2048]{2,0,1:T(8,128)S(1)} %get-tuple-element.18), channel_id=1, source_target_pairs={{0,1},{1,2},{2,3},{3,4},{4,5},{5,6},{6,7},{7,8},{8,9},{9,10},{10,1... | collective-permute-start | bytes 1179656 | tf_op jit(solution)/shard_map/ppermute | solution.py:20
  57.7 1.5 collective-permute-start.1
  59.2 6.3 %collective-permute-done = f32[8,6,2048]{2,0,1:T(8,128)S(1)} collective-permute-done((f32[8,6,2048]{2,0,1:T(8,128)S(1)}, f32[8,6,2048]{2,0,1:T(8,128)S(1)}, u32[]{:S(2)}, u32[]{:S(2)}) %collective-permute-start) | collective-permute-done | bytes 393248 | tf_op jit(solution)/shard_map/ppermute | solution.py:20
  65.5 3.8 %collective-permute-done.1 = f32[8,6,2048]{2,0,1:T(8,128)S(1)} collective-permute-done((f32[8,6,2048]{2,0,1:T(8,128)S(1)}, f32[8,6,2048]{2,0,1:T(8,128)S(1)}, u32[]{:S(2)}, u32[]{:S(2)}) %collective-permute-start.1) | collective-permute-done | bytes 393248 | tf_op jit(solution)/shard_map/ppermute | solution.py:21
  69.3 32.9 %fusion.4 = f32[8,64,2048]{2,0,1:T(8,128)} fusion(f32[8,64,2048]{2,0,1:T(8,128)} %multiply_add_fusion, f32[8,6,2048]{2,0,1:T(8,128)S(1)} %collective-permute-done.1, f32[8,6,2048]{2,0,1:T(8,128)S(1)} %collective-permute-done, f32[]{:T(128)} %bitcast.12, f32[]{:T(128)} %bitcast.11, f32[]{:T(128)} %bitcast.10, f32[]{:T(128)} %bitcast.9, f32[]{:T(128)} %bitcast.8, ...), kind=kLoop, calls=%fused_computation.29 | loop fusion | flops 39845888 | bytes 13369396 | tf_op jit(solution)/shard_map/sub | solution.py:52
  102.1 7.5 %copy.38 = f32[8,64,2048]{1,0,2:T(8,128)} copy(f32[8,64,2048]{2,0,1:T(8,128)} %fusion.4) | data formatting | bytes 8388608 | tf_op jit(solution)/shard_map/sub | solution.py:52
  109.6 9.8 %reshape.84 = f32[8,1,131072]{2,1,0:T(1,128)} reshape(f32[2048,8,64]{2,1,0:T(8,128)} %bitcast.46) | data formatting | bytes 8388608
  119.4 0.0 copy-start.1
  119.4 0.0 copy-start.2
  119.4 0.0 copy-start
  119.4 0.0 copy-start.3
  119.4 0.0 copy-start.4
  119.5 6.5 %all-to-all-start = ((f32[8,1,131072]{2,1,0:T(1,128)}), f32[8,1,131072]{2,1,0:T(1,128)}, u32[]{:S(2)}, u32[]{:S(2)}) async-start(f32[8,1,131072]{2,1,0:T(1,128)} %reshape.84), calls=%async_computation | async-start | bytes 8388608 | tf_op jit(solution)/shard_map/all_to_all | solution.py:54
  125.9 0.0 copy-done.1
  125.9 0.0 copy-done.2
  125.9 0.2 convert_reduce_fusion
  126.1 0.2 fusion.58
  126.3 0.8 all_to_all.28
  127.1 0.0 copy-done
  127.1 0.7 fusion.74
  127.8 0.0 copy-done.3
  127.8 0.0 copy-done.4
  127.8 0.1 fusion.63
  127.9 46.9 %all-to-all-done = f32[8,1,131072]{2,1,0:T(1,128)} async-done(((f32[8,1,131072]{2,1,0:T(1,128)}), f32[8,1,131072]{2,1,0:T(1,128)}, u32[]{:S(2)}, u32[]{:S(2)}) %all-to-all-start) | async-done | bytes 4194336 | tf_op jit(solution)/shard_map/all_to_all | solution.py:54
  174.8 10.6 %all-to-all-start.1 = ((f32[128,1,2]{2,1,0:T(1,128)}), f32[128,1,2]{2,1,0:T(1,128)S(1)}, u32[]{:S(2)}, u32[]{:S(2)}) async-start(f32[128,1,2]{2,1,0:T(1,128)} %bitcast.31), calls=%async_computation.1 | async-start | bytes 131072 | tf_op jit(solution)/shard_map/all_to_all | solution.py:83
  185.4 0.5 broadcast.84
  185.9 13.8 %reduce.3 = f32[8,131072]{1,0:T(8,128)} reduce(f32[8,1,131072]{2,1,0:T(1,128)} %all-to-all-done, f32[]{:T(128)} %broadcast.84), dimensions={1}, to_apply=%all_to_all.24.reduce_sub_computation | reduce | bytes 8388612 | tf_op jit(solution)/shard_map/all_to_all | solution.py:54
  199.7 8.7 %reshape.85 = f32[2048,8,64]{2,1,0:T(8,128)} reshape(f32[8,131072]{1,0:T(8,128)} %reduce.3) | data formatting | bytes 8388608
  208.4 6.8 %copy.39 = f32[8,8,64,256]{3,2,1,0:T(8,128)} copy(f32[8,8,64,256]{2,1,3,0:T(8,128)} %bitcast.47) | data formatting | bytes 8388608 | tf_op jit(solution)/shard_map/all_to_all | solution.py:54
  215.1 12.2 %add_subtract_fusion = f32[64,64,256]{2,1,0:T(8,128)S(1)} fusion(f32[64,64,256]{2,1,0:T(8,128)} %bitcast.48, f32[]{:T(128)} %bitcast.20, f32[]{:T(128)} %bitcast.19, f32[]{:T(128)} %bitcast.18, f32[]{:T(128)} %bitcast.17, f32[]{:T(128)} %bitcast.16), kind=kLoop, calls=%fused_computation.72 | loop fusion | flops 10485760 | bytes 8388628 | tf_op jit(solution)/shard_map/sub | solution.py:43
  227.3 6.6 %fusion.38 = f32[64,64,256]{2,1,0:T(8,128)} fusion(f32[64,64,256]{2,1,0:T(8,128)S(1)} %add_subtract_fusion, f32[]{:T(128)} %bitcast.25, f32[]{:T(128)} %bitcast.24, f32[]{:T(128)} %bitcast.23, f32[]{:T(128)} %bitcast.22, f32[]{:T(128)} %bitcast.21), kind=kLoop, calls=%fused_computation.63 | loop fusion | flops 10485760 | bytes 8388628 | tf_op jit(solution)/shard_map/sub | solution.py:43
  233.9 5.8 %reshape.61 = f32[64,64,2,128]{3,2,1,0:T(2,128)} reshape(f32[64,64,256]{2,1,0:T(8,128)} %fusion.38) | data formatting | bytes 8388608 | tf_op jit(solution)/shard_map/reshape | solution.py:57
  239.7 6.5 %copy.41 = f32[64,64,2,128]{3,0,2,1:T(8,128)} copy(f32[64,64,2,128]{3,2,1,0:T(2,128)} %reshape.61) | data formatting | bytes 8388608 | tf_op jit(solution)/shard_map/reshape | solution.py:57
  246.2 5.0 %gather_fusion = f32[128,64,128]{2,1,0:T(8,128)} fusion(f32[64,64,2,128]{3,0,2,1:T(8,128)} %copy.41, s32[128]{0:T(128)S(1)} %fusion.67), kind=kCustom, calls=%fused_computation | custom fusion | bytes 8389632 | tf_op jit(solution)/shard_map/gather | solution.py:58
  251.3 3.4 %multiply_reduce_fusion = f32[128,64]{1,0:T(8,128)S(1)} fusion(f32[128,64,128]{2,1,0:T(8,128)} %gather_fusion, f32[128,128]{1,0:T(8,128)S(1)} %fusion.63), kind=kLoop, calls=%fused_computation.71 | loop fusion | flops 2088960 | bytes 4292608 | tf_op jit(solution)/shard_map/reduce_sum | solution.py:61
  254.6 0.4 fusion.57
  255.0 0.8 reshape.86
  255.8 0.0 all-to-all-done.1
  255.8 9.8 %all-to-all-start.2 = ((f32[128,1,128]{2,1,0:T(1,128)}), f32[128,1,128]{2,1,0:T(1,128)S(1)}, u32[]{:S(2)}, u32[]{:S(2)}) async-start(f32[128,1,128]{2,1,0:T(1,128)} %reshape.86), calls=%async_computation.2 | async-start | bytes 131072 | tf_op jit(solution)/shard_map/all_to_all | solution.py:76
  265.6 0.8 reduce_sum.52
  266.4 8.9 %all-to-all-done.2 = f32[128,1,128]{2,1,0:T(1,128)S(1)} async-done(((f32[128,1,128]{2,1,0:T(1,128)}), f32[128,1,128]{2,1,0:T(1,128)S(1)}, u32[]{:S(2)}, u32[]{:S(2)}) %all-to-all-start.2) | async-done | bytes 65568 | tf_op jit(solution)/shard_map/all_to_all | solution.py:76
  275.2 0.8 reduce.4
  276.1 0.1 reshape.87
  276.2 0.2 multiply_reduce_fusion.1
  276.4 0.7 broadcast_divide_fusion
  277.1 1.2 fusion.76
  278.3 0.2 subtract_select_fusion
  278.5 0.7 copy.43
  (4 shorter events, 0.0 us)
Async XLA Ops:
  53.7 11.7 %collective-permute-start = (f32[8,6,2048]{2,0,1:T(8,128)S(1)}, f32[8,6,2048]{2,0,1:T(8,128)S(1)}, u32[]{:S(2)}, u32[]{:S(2)}) collective-permute-start(f32[8,6,2048]{2,0,1:T(8,128)S(1)} %get-tuple-element.18), channel_id=1, source_target_pairs={{0,1},{1,2},{2,3},{3,4},{4,5},{5,6},{6,7},{7,8},{8,9},{9,10},{10,1... | collective-permute-start | bytes 1179656 | tf_op jit(solution)/shard_map/ppermute | solution.py:20
  57.7 11.6 %collective-permute-start.1 = (f32[8,6,2048]{2,0,1:T(8,128)S(1)}, f32[8,6,2048]{2,0,1:T(8,128)S(1)}, u32[]{:S(2)}, u32[]{:S(2)}) collective-permute-start(f32[8,6,2048]{2,0,1:T(8,128)S(1)} %get-tuple-element.19), channel_id=1, source_target_pairs={{1,0},{2,1},{3,2},{4,3},{5,4},{6,5},{7,6},{8,7},{9,8},{10,9},{11,1... | collective-permute-start | bytes 1179656 | tf_op jit(solution)/shard_map/ppermute | solution.py:21
  119.4 6.5 %copy-start.1 = (s32[128]{0:T(128)S(1)}, s32[128]{0:T(128)}, u32[]{:S(2)}) copy-start(s32[128]{0:T(128)} %param.12) | copy-start | bytes 1540
  119.4 6.5 %copy-start.2 = (s32[128,1]{0,1:T(1,128)S(1)}, s32[128,1]{0,1:T(1,128)}, u32[]{:S(2)}) copy-start(s32[128,1]{0,1:T(1,128)} %param.13) | copy-start | bytes 1540
  119.4 7.7 %copy-start = (f32[2,5]{1,0:T(2,128)S(1)}, f32[2,5]{1,0:T(2,128)}, u32[]{:S(2)}) copy-start(f32[2,5]{1,0:T(2,128)} %param.9) | copy-start | bytes 124
  119.4 8.4 %copy-start.3 = (s32[128]{0:T(128)S(1)}, s32[128]{0:T(128)}, u32[]{:S(2)}) copy-start(s32[128]{0:T(128)} %param.11) | copy-start | bytes 1540
  119.4 8.4 %copy-start.4 = (s32[128]{0:T(128)S(1)}, s32[128]{0:T(128)}, u32[]{:S(2)}) copy-start(s32[128]{0:T(128)} %param.10) | copy-start | bytes 1540
  119.5 55.4 %all-to-all-start = ((f32[8,1,131072]{2,1,0:T(1,128)}), f32[8,1,131072]{2,1,0:T(1,128)}, u32[]{:S(2)}, u32[]{:S(2)}) async-start(f32[8,1,131072]{2,1,0:T(1,128)} %reshape.84), calls=%async_computation | async-start | bytes 8388608 | tf_op jit(solution)/shard_map/all_to_all | solution.py:54
  174.8 80.9 %all-to-all-start.1 = ((f32[128,1,2]{2,1,0:T(1,128)}), f32[128,1,2]{2,1,0:T(1,128)S(1)}, u32[]{:S(2)}, u32[]{:S(2)}) async-start(f32[128,1,2]{2,1,0:T(1,128)} %bitcast.31), calls=%async_computation.1 | async-start | bytes 131072 | tf_op jit(solution)/shard_map/all_to_all | solution.py:83
  255.8 19.5 %all-to-all-start.2 = ((f32[128,1,128]{2,1,0:T(1,128)}), f32[128,1,128]{2,1,0:T(1,128)S(1)}, u32[]{:S(2)}, u32[]{:S(2)}) async-start(f32[128,1,128]{2,1,0:T(1,128)} %reshape.86), calls=%async_computation.2 | async-start | bytes 131072 | tf_op jit(solution)/shard_map/all_to_all | solution.py:76
where the time goes:
time: 281 us; the launch traced here: 279 us
  other arithmetic  118 us (42%)
  waiting for transfers between devices  65.9 us (23%)
  local copies, waits for them, and re-layouts  62.2 us (22%)
  starting transfers between devices  32.2 us (11%)
    all_to_all x1, waiting for transfers between devices, shards(): lax.all_to_all(corrected, 'date', split_axis=2, concat_axis=0, tiled=True)  46.9 us
    add x1, other arithmetic, taps_pass(): summed + weights[k] * lax.slice_in_dim(padded, k, k + length, axis=axis_num)  42 us
    sub x1, other arithmetic, shards(): corrected = stack - taps_pass(rimmed, weights, 1, stack.shape[1])  32.9 us
    unnamed x16, local copies, waits for them, and re-layouts  26.8 us
    sub x2, other arithmetic, temporal_filter(): series = series - smooth_part  18.8 us
    all_to_all x1, other arithmetic, shards(): lax.all_to_all(corrected, 'date', split_axis=2, concat_axis=0, tiled=True)  13.8 us
    reshape x2, local copies, waits for them, and re-layouts, shards(): tile_view = residual.reshape(date_count, row_count, col_count // TILE, TILE)  12.3 us
    all_to_all x1, starting transfers between devices, shards(): lax.all_to_all(out_weight.reshape(devices_all, PAIR_CAP), ('date', 'strip...  10.6 us
  transfers between devices with their start and end apart: 5, of which 4 were waited for; matrix products, arithmetic and copies ran while one was open for 26% of the time, Pallas kernels for 0%

commit v1 on v0

--- a/solution.py
+++ b/solution.py
@@ -2,12 +2,19 @@
 import jax.numpy as jnp
 from jax import lax
 from jax.sharding import PartitionSpec as P
+from jax.lax import all_to_all, axis_size
 
 TILE = 128
 RADIUS = 6
 REACH = 2
 DILATION = 8
 PAIR_CAP = 2
+
+
+def _state_tracks(s0, axis_k, dim_at):
+    y = axis_size("date")
+    right_arr = jnp.stack(jnp.split(s0, y, axis_k), 0)
+    return jnp.concatenate(all_to_all(right_arr, "date", 0, 0), dim_at)
 
 
 def with_halo(value, sides, width):
@@ -50,9 +57,7 @@
     across = taps_pass(padded, weights, 2, stack.shape[2])
     rimmed = with_halo(across, (("strip", 1),), RADIUS)
     corrected = stack - taps_pass(rimmed, weights, 1, stack.shape[1])
-    residual = temporal_filter(
-        lax.all_to_all(corrected, "date", split_axis=2, concat_axis=0, tiled=True), temporal_taps
-    )
+    residual = temporal_filter(_state_tracks(corrected, axis_k=2, dim_at=0), temporal_taps)
     date_count, row_count, col_count = residual.shape
     tile_view = residual.reshape(date_count, row_count, col_count // TILE, TILE)
     picked = tile_view[:, foot_row, foot_tile, :]

time: 281 us -> 242 us (0.86)
  local copies, waits for them, and re-layouts: 62.2 us -> 29.6 us
  other arithmetic: 118 us -> 110 us
  waiting for transfers between devices: 65.9 us -> 68.8 us
    unnamed x16 -> x20, local copies, waits for them, and re-layouts: 26.8 us -> 7.48 us
    all_to_all x1 -> x0, other arithmetic: 13.8 us -> none  [shards(): lax.all_to_all(corrected, 'date', split_axis=2, concat_axis=0, tiled=True)]
    sub x1 -> x0, local copies, waits for them, and re-layouts: 7.48 us -> none  [shards(): corrected = stack - taps_pass(rimmed, weights, 1, stack.shape[1])]
    all_to_all x2 -> x1, local copies, waits for them, and re-layouts: 7.29 us -> 0.51 us  [shards(): lax.all_to_all(outgoing.reshape(devices_all, PAIR_CAP, date_count), ('dat...]
    sub x1, other arithmetic: 32.9 us -> 38.8 us  [shards(): corrected = stack - taps_pass(rimmed, weights, 1, stack.shape[1])]
    ppermute x1, waiting for transfers between devices: 6.26 us -> 9.24 us  [with_halo(): before = lax.ppermute(last, axis, up)]
  transfers between devices with their start and end apart: 5 -> 5, of which waited for: 4 -> 4; matrix products, arithmetic and copies ran while one was open for 26% -> 18% of each run, Pallas kernels for 0% -> 0%
where the time goes in v1:
time: 242 us; the launch traced here: 241 us
  other arithmetic  110 us (45%)
  waiting for transfers between devices  68.8 us (28%)
  starting transfers between devices  32.1 us (13%)
  local copies, waits for them, and re-layouts  29.6 us (12%)
    all_to_all x1, waiting for transfers between devices, _state_tracks(): return jnp.concatenate(all_to_all(right_arr, 'date', 0, 0), dim_at)  46.9 us
    add x1, other arithmetic, taps_pass(): summed + weights[k] * lax.slice_in_dim(padded, k, k + length, axis=axis_num)  41.8 us
    sub x1, other arithmetic, shards(): corrected = stack - taps_pass(rimmed, weights, 1, stack.shape[1])  38.8 us
    sub x2, other arithmetic, temporal_filter(): series = series - smooth_part  18.8 us
    reshape x2, local copies, waits for them, and re-layouts, shards(): tile_view = residual.reshape(date_count, row_count, col_count // TILE, TILE)  12.3 us
    all_to_all x1, starting transfers between devices, shards(): lax.all_to_all(out_weight.reshape(devices_all, PAIR_CAP), ('date', 'strip...  10.5 us
    all_to_all x1, starting transfers between devices, shards(): lax.all_to_all(outgoing.reshape(devices_all, PAIR_CAP, date_count), ('dat...  9.76 us
    ppermute x1, waiting for transfers between devices, with_halo(): before = lax.ppermute(last, axis, up)  9.24 us
  transfers between devices with their start and end apart: 5, of which 4 were waited for; matrix products, arithmetic and copies ran while one was open for 18% of the time, Pallas kernels for 0%

profile of v1, /device:TPU:1, one launch (start us, length us, event | category | flops | bytes accessed | tf_op | source)
XLA Modules:
  0.0 241.4 jit_solution(9381639222899346599)
XLA Ops:
  0.6 1.3 reduce_sum.47
  1.9 1.3 broadcast_divide_fusion.1
  3.2 0.7 fusion.83
  3.9 41.8 %multiply_add_fusion = f32[8,64,2048]{2,1,0:T(8,128)} fusion(f32[8,64,2048]{2,1,0:T(8,128)} %param.7, f32[]{:T(128)} %bitcast.12, f32[]{:T(128)} %bitcast.11, f32[]{:T(128)} %bitcast.10, f32[]{:T(128)} %bitcast.9, f32[]{:T(128)} %bitcast.8, f32[]{:T(128)} %bitcast.7, f32[]{:T(128)} %bitcast.6, f32[]{:T(128)} %bitcast.5, f32[]{:T(128)} %bitcast.4, ...), kind=kLoop, calls=%fused_computation.79 | loop fusion | flops 26214400 | bytes 8388660 | tf_op jit(solution)/shard_map/add | solution.py:36
  45.7 1.3 fusion.81
  47.0 4.0 %collective-permute-start = (f32[8,6,2048]{2,1,0:T(8,128)S(1)}, f32[8,6,2048]{2,1,0:T(8,128)S(1)}, u32[]{:S(2)}, u32[]{:S(2)}) collective-permute-start(f32[8,6,2048]{2,1,0:T(8,128)S(1)} %get-tuple-element.15), channel_id=1, source_target_pairs={{0,1},{1,2},{2,3},{3,4},{4,5},{5,6},{6,7},{7,8},{8,9},{9,10},{10,1... | collective-permute-start | bytes 1179656 | tf_op jit(solution)/shard_map/ppermute | solution.py:27
  50.9 1.3 collective-permute-start.1
  52.2 9.2 %collective-permute-done = f32[8,6,2048]{2,1,0:T(8,128)S(1)} collective-permute-done((f32[8,6,2048]{2,1,0:T(8,128)S(1)}, f32[8,6,2048]{2,1,0:T(8,128)S(1)}, u32[]{:S(2)}, u32[]{:S(2)}) %collective-permute-start) | collective-permute-done | bytes 393248 | tf_op jit(solution)/shard_map/ppermute | solution.py:27
  61.5 3.8 %collective-permute-done.1 = f32[8,6,2048]{2,1,0:T(8,128)S(1)} collective-permute-done((f32[8,6,2048]{2,1,0:T(8,128)S(1)}, f32[8,6,2048]{2,1,0:T(8,128)S(1)}, u32[]{:S(2)}, u32[]{:S(2)}) %collective-permute-start.1) | collective-permute-done | bytes 393248 | tf_op jit(solution)/shard_map/ppermute | solution.py:28
  65.3 38.8 %fusion.4 = f32[8,64,2048]{2,1,0:T(8,128)S(1)} fusion(f32[8,64,2048]{2,1,0:T(8,128)} %param.7, f32[8,64,2048]{2,1,0:T(8,128)} %multiply_add_fusion, f32[8,6,2048]{2,1,0:T(8,128)S(1)} %collective-permute-done.1, f32[8,6,2048]{2,1,0:T(8,128)S(1)} %collective-permute-done, f32[]{:T(128)} %bitcast.12, f32[]{:T(128)} %bitcast.11, f32[]{:T(128)} %bitcast.10, ...), kind=kLoop, calls=%fused_computation.29 | loop fusion | flops 39845888 | bytes 13369396 | tf_op jit(solution)/shard_map/sub | solution.py:59
  104.1 0.8 fusion.64
  104.9 0.8 fusion.63
  105.8 0.8 fusion.62
  106.6 0.8 fusion.61
  107.4 0.8 fusion.60
  108.3 0.8 fusion.59
  109.1 0.8 fusion.58
  109.9 0.8 fusion.57
  110.8 0.0 copy-start.1
  110.8 0.0 copy-start.2
  110.8 0.0 copy-start
  110.8 0.0 copy-start.3
  110.8 0.0 copy-start.4
  110.8 6.5 %all-to-all-start = ((f32[8,8,64,256]{3,2,1,0:T(8,128)}), f32[8,8,64,256]{3,2,1,0:T(8,128)}, u32[]{:S(2)}, u32[]{:S(2)}) async-start(f32[8,8,64,256]{3,2,1,0:T(8,128)} %fusion.57), calls=%async_computation | async-start | bytes 8388608 | tf_op jit(solution)/shard_map/all_to_all | solution.py:17
  117.3 0.0 copy-done.1
  117.3 0.0 copy-done.2
  117.3 0.2 convert_reduce_fusion
  117.5 0.2 fusion.66
  117.7 0.8 all_to_all.15
  118.5 0.0 copy-done
  118.5 0.7 fusion.82
  119.2 0.0 copy-done.3
  119.2 0.0 copy-done.4
  119.2 0.1 fusion.71
  119.3 46.9 %all-to-all-done = f32[8,8,64,256]{3,2,1,0:T(8,128)} async-done(((f32[8,8,64,256]{3,2,1,0:T(8,128)}), f32[8,8,64,256]{3,2,1,0:T(8,128)}, u32[]{:S(2)}, u32[]{:S(2)}) %all-to-all-start) | async-done | bytes 4194336 | tf_op jit(solution)/shard_map/all_to_all | solution.py:17
  166.2 10.5 %all-to-all-start.1 = ((f32[128,1,2]{2,1,0:T(1,128)}), f32[128,1,2]{2,1,0:T(1,128)S(1)}, u32[]{:S(2)}, u32[]{:S(2)}) async-start(f32[128,1,2]{2,1,0:T(1,128)} %bitcast.37), calls=%async_computation.1 | async-start | bytes 131072 | tf_op jit(solution)/shard_map/all_to_all | solution.py:88
  176.7 12.1 %add_subtract_fusion = f32[64,64,256]{2,1,0:T(8,128)S(1)} fusion(f32[64,64,256]{2,1,0:T(8,128)} %bitcast.21, f32[]{:T(128)} %bitcast.26, f32[]{:T(128)} %bitcast.25, f32[]{:T(128)} %bitcast.24, f32[]{:T(128)} %bitcast.23, f32[]{:T(128)} %bitcast.22), kind=kLoop, calls=%fused_computation.72 | loop fusion | flops 10485760 | bytes 8388628 | tf_op jit(solution)/shard_map/sub | solution.py:50
  188.9 6.7 %fusion.38 = f32[64,64,256]{2,1,0:T(8,128)} fusion(f32[64,64,256]{2,1,0:T(8,128)S(1)} %add_subtract_fusion, f32[]{:T(128)} %bitcast.31, f32[]{:T(128)} %bitcast.30, f32[]{:T(128)} %bitcast.29, f32[]{:T(128)} %bitcast.28, f32[]{:T(128)} %bitcast.27), kind=kLoop, calls=%fused_computation.63 | loop fusion | flops 10485760 | bytes 8388628 | tf_op jit(solution)/shard_map/sub | solution.py:50
  195.6 5.8 %reshape.65 = f32[64,64,2,128]{3,2,1,0:T(2,128)} reshape(f32[64,64,256]{2,1,0:T(8,128)} %fusion.38) | data formatting | bytes 8388608 | tf_op jit(solution)/shard_map/reshape | solution.py:62
  201.3 6.5 %copy.20 = f32[64,64,2,128]{3,0,2,1:T(8,128)} copy(f32[64,64,2,128]{3,2,1,0:T(2,128)} %reshape.65) | data formatting | bytes 8388608 | tf_op jit(solution)/shard_map/reshape | solution.py:62
  207.9 5.0 %gather_fusion = f32[128,64,128]{2,1,0:T(8,128)} fusion(f32[64,64,2,128]{3,0,2,1:T(8,128)} %copy.20, s32[128]{0:T(128)S(1)} %fusion.75), kind=kCustom, calls=%fused_computation | custom fusion | bytes 8389632 | tf_op jit(solution)/shard_map/gather | solution.py:63
  212.9 3.4 %multiply_reduce_fusion = f32[128,64]{1,0:T(8,128)S(1)} fusion(f32[128,64,128]{2,1,0:T(8,128)} %gather_fusion, f32[128,128]{1,0:T(8,128)S(1)} %fusion.71), kind=kLoop, calls=%fused_computation.71 | loop fusion | flops 2088960 | bytes 4292608 | tf_op jit(solution)/shard_map/reduce_sum | solution.py:66
  216.3 0.4 fusion.65
  216.6 0.8 reshape.88
  217.4 0.0 all-to-all-done.1
  217.4 9.8 %all-to-all-start.2 = ((f32[128,1,128]{2,1,0:T(1,128)}), f32[128,1,128]{2,1,0:T(1,128)S(1)}, u32[]{:S(2)}, u32[]{:S(2)}) async-start(f32[128,1,128]{2,1,0:T(1,128)} %reshape.88), calls=%async_computation.2 | async-start | bytes 131072 | tf_op jit(solution)/shard_map/all_to_all | solution.py:81
  227.2 0.8 reduce_sum.52
  228.0 8.9 %all-to-all-done.2 = f32[128,1,128]{2,1,0:T(1,128)S(1)} async-done(((f32[128,1,128]{2,1,0:T(1,128)}), f32[128,1,128]{2,1,0:T(1,128)S(1)}, u32[]{:S(2)}, u32[]{:S(2)}) %all-to-all-start.2) | async-done | bytes 65568 | tf_op jit(solution)/shard_map/all_to_all | solution.py:81
  236.9 0.5 broadcast.84
  237.4 0.8 reduce.3
  238.2 0.1 reshape.89
  238.3 0.2 multiply_reduce_fusion.1
  238.6 0.7 broadcast_divide_fusion
  239.3 1.2 fusion.84
  240.5 0.2 subtract_select_fusion
  240.7 0.7 copy.22
  (4 shorter events, 0.0 us)
Async XLA Ops:
  47.0 14.5 %collective-permute-start = (f32[8,6,2048]{2,1,0:T(8,128)S(1)}, f32[8,6,2048]{2,1,0:T(8,128)S(1)}, u32[]{:S(2)}, u32[]{:S(2)}) collective-permute-start(f32[8,6,2048]{2,1,0:T(8,128)S(1)} %get-tuple-element.15), channel_id=1, source_target_pairs={{0,1},{1,2},{2,3},{3,4},{4,5},{5,6},{6,7},{7,8},{8,9},{9,10},{10,1... | collective-permute-start | bytes 1179656 | tf_op jit(solution)/shard_map/ppermute | solution.py:27
  50.9 14.4 %collective-permute-start.1 = (f32[8,6,2048]{2,1,0:T(8,128)S(1)}, f32[8,6,2048]{2,1,0:T(8,128)S(1)}, u32[]{:S(2)}, u32[]{:S(2)}) collective-permute-start(f32[8,6,2048]{2,1,0:T(8,128)S(1)} %get-tuple-element.16), channel_id=1, source_target_pairs={{1,0},{2,1},{3,2},{4,3},{5,4},{6,5},{7,6},{8,7},{9,8},{10,9},{11,1... | collective-permute-start | bytes 1179656 | tf_op jit(solution)/shard_map/ppermute | solution.py:28
  110.8 6.5 %copy-start.1 = (s32[128]{0:T(128)S(1)}, s32[128]{0:T(128)}, u32[]{:S(2)}) copy-start(s32[128]{0:T(128)} %param.12) | copy-start | bytes 1540
  110.8 6.5 %copy-start.2 = (s32[128,1]{0,1:T(1,128)S(1)}, s32[128,1]{0,1:T(1,128)}, u32[]{:S(2)}) copy-start(s32[128,1]{0,1:T(1,128)} %param.13) | copy-start | bytes 1540
  110.8 7.7 %copy-start = (f32[2,5]{1,0:T(2,128)S(1)}, f32[2,5]{1,0:T(2,128)}, u32[]{:S(2)}) copy-start(f32[2,5]{1,0:T(2,128)} %param.9) | copy-start | bytes 124
  110.8 8.4 %copy-start.3 = (s32[128]{0:T(128)S(1)}, s32[128]{0:T(128)}, u32[]{:S(2)}) copy-start(s32[128]{0:T(128)} %param.11) | copy-start | bytes 1540
  110.8 8.4 %copy-start.4 = (s32[128]{0:T(128)S(1)}, s32[128]{0:T(128)}, u32[]{:S(2)}) copy-start(s32[128]{0:T(128)} %param.10) | copy-start | bytes 1540
  110.8 55.4 %all-to-all-start = ((f32[8,8,64,256]{3,2,1,0:T(8,128)}), f32[8,8,64,256]{3,2,1,0:T(8,128)}, u32[]{:S(2)}, u32[]{:S(2)}) async-start(f32[8,8,64,256]{3,2,1,0:T(8,128)} %fusion.57), calls=%async_computation | async-start | bytes 8388608 | tf_op jit(solution)/shard_map/all_to_all | solution.py:17
  166.2 51.2 %all-to-all-start.1 = ((f32[128,1,2]{2,1,0:T(1,128)}), f32[128,1,2]{2,1,0:T(1,128)S(1)}, u32[]{:S(2)}, u32[]{:S(2)}) async-start(f32[128,1,2]{2,1,0:T(1,128)} %bitcast.37), calls=%async_computation.1 | async-start | bytes 131072 | tf_op jit(solution)/shard_map/all_to_all | solution.py:88
  217.4 19.5 %all-to-all-start.2 = ((f32[128,1,128]{2,1,0:T(1,128)}), f32[128,1,128]{2,1,0:T(1,128)S(1)}, u32[]{:S(2)}, u32[]{:S(2)}) async-start(f32[128,1,128]{2,1,0:T(1,128)} %reshape.88), calls=%async_computation.2 | async-start | bytes 131072 | tf_op jit(solution)/shard_map/all_to_all | solution.py:81
